TPU v7x, 256 devices: a whole 4x4x8 slice. The times are simulated.
256 devices in a mesh: ctx: 32 (over y, z), tp: 8 (over x, core).
Axes of the slice: x: 4, y: 4, z: 8, core: 2. Of those that a mesh axis runs over, the one named last changes fastest.
Arguments:
- ssm_inputs: bfloat16 [8192, 8192], P('ctx', 'tp'), may hold values from -4 to 4
- state_maps: bfloat16 [8192, 8, 256], P('ctx', 'tp'), may hold values from -4 to 4
- ssm_gates: bfloat16 [8192, 8192], P('ctx', 'tp'), may hold values from -4 to 4
- time_steps: float32 [128, 8192], P('tp', 'ctx'), may hold values from -5 to 512
- log_rates: float32 [128], P('tp'), may hold values from -12 to 1
- skip_gain: float32 [128], P('tp'), may hold values from 0.5 to 2
- conv_inputs: bfloat16 [4, 8192], P(None, 'tp'), may hold values from -3 to 3
- conv_maps: bfloat16 [4, 8, 256], P(None, 'tp'), may hold values from -3 to 3
- norm_gain: float32 [8192], P('tp'), may hold values from 0.1 to 1.9
- out_weight: bfloat16 [8192, 4096], P('tp'), may hold values from -0.0625 to 0.0625
- queries: bfloat16 [8192, 8192], P('ctx', 'tp'), may hold values from -5 to 5
- attention_keys: bfloat16 [8192, 1024], P('ctx', 'tp'), may hold values from -5 to 5
- values: bfloat16 [8192, 1024], P('ctx', 'tp'), may hold values from -4 to 4
Outputs:
- ssm_out: bfloat16 [8192, 4096], P(('ctx', 'tp'))
- attn_out: bfloat16 [8192, 8192], P('ctx', 'tp')
All inputs are finite; a program needn't handle non-finite values.
Results may differ from a plain program's by a relative error of at most 0.03.
Values may be sent and summed in bfloat16 or wider, within the bound.
No kernel may reach another device: no remote copies, remote signals or barrier semaphores. Data moves between devices by JAX's collectives and lax.ppermute only.
A program may use at most 128 MiB of HBM per device.

v0:
```python
import jax
import jax.numpy as jnp
from jax import lax
from jax.sharding import PartitionSpec as P

QUERY_HEADS = 64
KEY_VALUE_HEADS = 8
HEAD_SIZE = 128


def passed_along(shard, axis, by):
    size = lax.axis_size(axis)
    pairs = [(i, i + by) for i in range(size) if 0 <= i + by < size]
    return lax.ppermute(shard, axis, pairs)


def prefix_2(shard, axis, join, neutral):
    place = lax.axis_index(axis)
    gathered = jax.tree.map(
        lambda a, kind: lax.all_gather(a.astype(kind), axis), shard, (jnp.bfloat16, jnp.bfloat16)
    )
    state = jax.tree.map(lambda a, e: jnp.zeros_like(a) + jnp.asarray(e, a.dtype), shard, neutral)

    def one(step, state):
        return join(
            state,
            jax.tree.map(
                lambda a, own: lax.dynamic_index_in_dim(a, step, 0, False).astype(own.dtype),
                gathered,
                shard,
            ),
        )

    return lax.fori_loop(0, place, one, state)


def conv_silu(extended, conv_taps, tok_rows):
    summed = jnp.zeros((tok_rows,) + extended.shape[1:], jnp.float32)
    for tap_index in range(conv_taps.shape[0]):
        summed = summed + conv_taps[tap_index].astype(jnp.float32) * extended[
            tap_index : tap_index + tok_rows
        ].astype(jnp.float32)
    return jax.nn.silu(summed).astype(jnp.bfloat16)


def per_device(
    ssm_inputs,
    state_maps,
    ssm_gates,
    time_steps,
    log_rates,
    skip_gain,
    conv_inputs,
    conv_maps,
    norm_gain,
    out_weight,
    queries,
    attention_keys,
    values,
):
    tok_rows = ssm_inputs.shape[0]
    tap_count = conv_inputs.shape[0]
    groups_here = state_maps.shape[1]
    state_size = state_maps.shape[2] // 2
    heads_here = log_rates.shape[0]
    per_group = heads_here // groups_here
    head_dim = ssm_inputs.shape[1] // heads_here
    my_index = lax.axis_index("ctx")
    lead_inputs, lead_maps = passed_along(
        (ssm_inputs[tok_rows - tap_count + 1 :], state_maps[tok_rows - tap_count + 1 :]), "ctx", 1
    )
    mixed_inputs = conv_silu(
        jnp.concatenate([lead_inputs, ssm_inputs], axis=0), conv_inputs, tok_rows
    )
    mixed_maps = conv_silu(jnp.concatenate([lead_maps, state_maps], axis=0), conv_maps, tok_rows)
    input_heads = mixed_inputs.reshape(tok_rows, groups_here, per_group, head_dim)
    b_maps = mixed_maps[:, :, :state_size]
    c_maps = mixed_maps[:, :, state_size:]
    step_sizes = jax.nn.softplus(time_steps).reshape(groups_here, per_group, tok_rows)
    decline_rate = -jnp.exp(log_rates).reshape(groups_here, per_group)
    running_log = jnp.cumsum(step_sizes * decline_rate[:, :, None], axis=2)
    map_products = jnp.einsum("tgn,sgn->gts", c_maps, b_maps, preferred_element_type=jnp.float32)
    token_location = jnp.arange(tok_rows)
    causal = token_location[:, None] >= token_location[None, :]
    log_gap = running_log[:, :, :, None] - running_log[:, :, None, :]
    decay_table = jnp.where(causal, jnp.exp(jnp.minimum(log_gap, 0.0)), 0.0)
    mixer = (map_products[:, None] * decay_table * step_sizes[:, :, None, :]).astype(jnp.bfloat16)
    inner_part = jnp.einsum(
        "gjts,sgjp->tgjp", mixer, input_heads, preferred_element_type=jnp.float32
    )
    inputs_float = input_heads.astype(jnp.float32)
    tail_weight = jnp.exp(running_log[:, :, -1:] - running_log) * step_sizes
    weighted = (jnp.transpose(tail_weight, (2, 0, 1))[..., None] * inputs_float).astype(
        jnp.bfloat16
    )
    block_state = jnp.einsum("sgjp,sgn->gjpn", weighted, b_maps, preferred_element_type=jnp.float32)
    block_decay = running_log[:, :, -1]

    def combine(earlier, later):
        return (earlier[0] + later[0], jnp.exp(later[0])[:, :, None, None] * earlier[1] + later[1])

    prefix = prefix_2(
        (block_decay, block_state),
        "ctx",
        combine,
        (jnp.zeros_like(block_decay), jnp.zeros_like(block_state)),
    )
    entering = prefix[1]
    carried = jnp.einsum(
        "tgn,gjpn->tgjp", c_maps.astype(jnp.float32), entering, precision=lax.Precision.HIGHEST
    )
    outside = jnp.transpose(jnp.exp(running_log), (2, 0, 1))[..., None] * carried
    ssm_output = (
        inner_part
        + outside
        + skip_gain.reshape(groups_here, per_group)[None, :, :, None] * inputs_float
    )
    channel_count = per_group * head_dim
    gated = ssm_output.reshape(tok_rows, groups_here, channel_count) * jax.nn.silu(
        ssm_gates.reshape(tok_rows, groups_here, channel_count).astype(jnp.float32)
    )
    mean_square = jnp.mean(gated * gated, axis=2, keepdims=True)
    normed = (
        (gated * lax.rsqrt(mean_square + 1e-05)).reshape(tok_rows, groups_here * channel_count)
        * norm_gain
    ).astype(jnp.bfloat16)
    ssm_out = lax.psum_scatter(
        jnp.dot(normed, out_weight, preferred_element_type=jnp.float32).astype(jnp.bfloat16),
        "tp",
        scatter_dimension=0,
        tiled=True,
    )
    kv_heads = attention_keys.shape[1] // HEAD_SIZE
    shared_heads = QUERY_HEADS // KEY_VALUE_HEADS
    score_scale = HEAD_SIZE ** (-0.5)
    query_pos = my_index * tok_rows + token_location
    query_heads = queries.reshape(tok_rows, kv_heads, shared_heads, HEAD_SIZE)
    block_rows = tok_rows // 4
    first_key = jnp.int32(0)
    key_block = lax.all_gather(attention_keys, "ctx", axis=0, tiled=True)
    value_block = lax.all_gather(values, "ctx", axis=0, tiled=True)
    key_count = key_block.shape[0]
    key_head_rows = key_block.reshape(key_count, kv_heads, HEAD_SIZE)
    value_head_rows = value_block.reshape(key_count, kv_heads, HEAD_SIZE)
    key_pos = jnp.arange(key_count)
    peaks = jnp.full((kv_heads, shared_heads, tok_rows), -1e30, jnp.float32)
    totals = jnp.zeros((kv_heads, shared_heads, tok_rows), jnp.float32)
    sums = jnp.zeros((kv_heads, shared_heads, tok_rows, HEAD_SIZE), jnp.float32)
    new_parts = []
    for current_block_index in range(4):
        row_lower = current_block_index * block_rows
        row_upper = row_lower + block_rows
        query_tile_block = query_heads[row_lower:row_upper]
        block_pos = query_pos[row_lower:row_upper]
        old_state = (
            peaks[:, :, row_lower:row_upper],
            totals[:, :, row_lower:row_upper],
            sums[:, :, row_lower:row_upper],
        )

        def update(old_part, query_tile_block=query_tile_block, block_pos=block_pos):
            old_peak, old_total, old_sum = old_part
            scores = (
                jnp.einsum(
                    "bgrd,kgd->grbk",
                    query_tile_block,
                    key_head_rows,
                    preferred_element_type=jnp.float32,
                )
                * score_scale
            )
            allowed = key_pos[None, :] <= block_pos[:, None]
            scores = jnp.where(allowed, scores, -1e30)
            new_peak = jnp.maximum(old_peak, jnp.max(scores, axis=3))
            weights = jnp.where(allowed, jnp.exp(scores - new_peak[..., None]), 0.0)
            new_total = jnp.sum(weights, axis=3)
            new_sum = jnp.einsum(
                "grbk,kgd->grbd",
                weights.astype(jnp.bfloat16),
                value_head_rows,
                preferred_element_type=jnp.float32,
            )
            return (new_peak, new_total, new_sum)

        def unchanged(old_part):
            return old_part

        new_parts.append(
            lax.cond(block_pos[block_rows - 1] >= first_key, update, unchanged, old_state)
        )
    peaks, totals, sums = tuple(
        (
            jnp.concatenate([block_part[member] for block_part in new_parts], axis=2)
            for member in range(3)
        )
    )
    attended = sums / totals[..., None]
    attn_out = (
        jnp.transpose(attended, (2, 0, 1, 3))
        .reshape(tok_rows, kv_heads * shared_heads * HEAD_SIZE)
        .astype(jnp.bfloat16)
    )
    return (ssm_out, attn_out)


def solution(mesh):
    placed = (
        P("ctx", "tp"),
        P("ctx", "tp", None),
        P("ctx", "tp"),
        P("tp", "ctx"),
        P("tp"),
        P("tp"),
        P(None, "tp"),
        P(None, "tp", None),
        P("tp"),
        P("tp", None),
        P("ctx", "tp"),
        P("ctx", "tp"),
        P("ctx", "tp"),
    )
    return jax.shard_map(
        per_device,
        mesh=mesh,
        in_specs=placed,
        out_specs=(P(("ctx", "tp"), None), P("ctx", "tp")),
        check_vma=False,
    )
```

profile of v0, /device:TPU:4, one launch (start us, length us, event | category | flops | bytes accessed | tf_op | source)
XLA Modules:
  0.0 351.8 jit_solution(560110108480496360)
XLA Ops:
  8.2 3.8 %collective-permute-start = (bf16[3,1024]{0,1:T(8,128)(2,1)S(1)}, bf16[3,1024]{0,1:T(8,128)(2,1)S(1)}, u32[]{:S(2)}, u32[]{:S(2)}) collective-permute-start(bf16[3,1024]{0,1:T(8,128)(2,1)S(1)} %copy.76), channel_id=1, source_target_pairs={{0,8},{8,16},{16,24},{24,32},{32,40},{40,48},{48,56},{56,64},{64,7... | collective-permute-start | bytes 18440 | tf_op jit(solution)/shard_map/ppermute | solution.py:14
  12.7 3.8 %collective-permute-start.1 = (bf16[3,1,256]{2,0,1:T(4,128)(2,1)S(1)}, bf16[3,1,256]{2,0,1:T(4,128)(2,1)S(1)}, u32[]{:S(2)}, u32[]{:S(2)}) collective-permute-start(bf16[3,1,256]{2,0,1:T(4,128)(2,1)S(1)} %slice.125), channel_id=1, source_target_pairs={{0,8},{8,16},{16,24},{24,32},{32,40},{40,48},{48,56},{56,64},{64,7... | collective-permute-start | bytes 4616 | tf_op jit(solution)/shard_map/ppermute | solution.py:14
  19.0 0.9 slice_convert_fusion.3
  20.7 0.8 slice_convert_fusion.7
  21.6 1.2 copy.77
  22.8 1.4 multiply_convert_fusion.7
  24.3 1.5 fusion.96
  25.7 1.0 convolution_convert_fusion.1
  28.3 40.3 %all-gather = bf16[32,16,1]{1,2,0:T(2,128)(2,1)S(1)} all-gather(bf16[1,16,1]{1,2,0:T(2,128)(2,1)S(1)} %slice.213), channel_id=2, replica_groups=mesh['ctx'=32,'tp'=8] {'ctx'}, dimensions={0}, use_global_device_ids=true | all-gather | bytes 1056 | tf_op jit(solution)/shard_map/all_gather | solution.py:20
  68.9 1.3 copy.88
  70.4 1.4 fusion.87
  71.8 54.2 %all-gather.10.cloned.1.call-done = bf16[512,64,128]{2,1,0:T(8,128)(2,1)} async-done(((bf16[16,64,128]{2,1,0:T(8,128)(2,1)}), bf16[512,64,128]{2,1,0:T(8,128)(2,1)}) %all-gather.10.cloned.1.call-update) | async-done | bytes 8388624 | tf_op jit(solution)/shard_map/all_gather | solution.py:20
  127.0 7.2 %convolution_convert_fusion = bf16[256,4096]{1,0:T(8,128)(2,1)} fusion(bf16[1024,4096]{1,0:T(8,128)(2,1)} %param.32, f32[256,1024]{0,1:T(8,128)S(1)} %get-tuple-element.171, f32[1024]{0:T(1024)S(1)} %copy-done, f32[256]{0:T(256)S(1)} %add_rsqrt_fusion), kind=kOutput, calls=%fused_computation.82 | convolution fusion | flops 2149318656 | bytes 11539456 | tf_op jit(solution)/shard_map/dot_general | solution.py:128
  137.2 66.5 %all-gather.6.cloned.1.call-done = bf16[8192,128]{1,0:T(8,128)(2,1)} async-done(((bf16[256,128]{1,0:T(8,128)(2,1)}), bf16[8192,128]{1,0:T(8,128)(2,1)}) %all-gather.6.cloned.1.call-update) | async-done | bytes 2097168 | tf_op jit(solution)/shard_map/all_gather | solution.py:140
  203.7 77.8 %all-gather.8.cloned.1.call-done = bf16[8192,128]{1,0:T(8,128)(2,1)} async-done(((bf16[256,128]{1,0:T(8,128)(2,1)}), bf16[8192,128]{1,0:T(8,128)(2,1)}) %all-gather.8.cloned.1.call-update) | async-done | bytes 2097168 | tf_op jit(solution)/shard_map/all_gather | solution.py:141
  281.5 15.4 %conditional.4 = (f32[1,8,64]{2,1,0:T(8,128)S(1)}, f32[1,8,64,128]{3,2,1,0:T(8,128)S(1)}) conditional(s32[]{:T(128)} %bitcast.73, () %tuple.48, (s32[8192]{0:T(1024)S(1)}, s32[256]{0:T(256)S(1)}, bf16[8192,1,128]{2,0,1:T(8,128)(2,1)}, bf16[256,1024]{1,0:T(8,128)(2,1)}, bf16[8192,1,128]{2,0,1:T(8,128)(2,1)}) %tuple.109), branch_computations={%region_6.7_spmd, %region_7.10_spmd} | conditional | flops 2202533376 | bytes 65450796 | solution.py:189
  281.8 4.8 %fusion = (f32[8,64]{1,0:T(8,128)S(1)}, f32[8192,64,8]{0,1,2:T(8,128)S(1)}) fusion(pred[64,8192]{1,0:T(8,128)(4,1)S(1)} %broadcast_compare_fusion, bf16[8192,1,128]{2,0,1:T(8,128)(2,1)} %get-tuple-element.97, bf16[256,1024]{1,0:T(8,128)(2,1)} %get-tuple-element.98), kind=kOutput, calls=%fused_computation.4 | convolution fusion | flops 1086324224 | bytes 19531776 | tf_op jit(solution)/shard_map/cond/branch_1_fun/bgrd,kgd->grbk/dot_general | solution.py:164
  286.7 4.7 %fusion.10 = f32[1,8,64,128]{3,2,1,0:T(8,128)S(1)} fusion(bf16[8192,1,128]{2,0,1:T(8,128)(2,1)S(1)} %copy-done.2, f32[8192,64,8]{0,1,2:T(8,128)S(1)} %get-tuple-element.179, f32[8,64]{1,0:T(8,128)S(1)} %broadcast_maximum_fusion, pred[64,8192]{1,0:T(8,128)(4,1)S(1)} %broadcast_compare_fusion), kind=kOutput, calls=%fused_computation.13 | convolution fusion | flops 1094713344 | bytes 19662848 | tf_op jit(solution)/shard_map/cond/branch_1_fun/grbk,kgd->grbd/dot_general | solution.py:177
  291.4 5.5 %fusion.2 = f32[8,64]{1,0:T(8,128)S(1)} fusion(f32[8192,64,8]{0,1,2:T(8,128)S(1)} %get-tuple-element.179, f32[8,64]{1,0:T(8,128)S(1)} %broadcast_maximum_fusion, pred[64,8192]{1,0:T(8,128)(4,1)S(1)} %broadcast_compare_fusion), kind=kLoop, calls=%fused_computation.6 | loop fusion | flops 20971008 | bytes 17305600 | tf_op jit(solution)/shard_map/cond/branch_1_fun/reduce_sum | solution.py:176
  296.9 15.5 %conditional.5 = (f32[1,8,64]{2,1,0:T(8,128)S(1)}, f32[1,8,64,128]{3,2,1,0:T(8,128)S(1)}) conditional(s32[]{:T(128)} %bitcast.76, () %tuple.50, (s32[8192]{0:T(1024)S(1)}, s32[256]{0:T(256)S(1)}, bf16[8192,1,128]{2,0,1:T(8,128)(2,1)}, bf16[256,1024]{1,0:T(8,128)(2,1)}, bf16[8192,1,128]{2,0,1:T(8,128)(2,1)}) %tuple.110), branch_computations={%region_10.11_spmd, %region_11.14_spmd} | conditional | flops 2202533376 | bytes 65450796 | solution.py:189
  297.3 4.9 %fusion.20 = (f32[8,64]{1,0:T(8,128)S(1)}, f32[8192,64,8]{0,1,2:T(8,128)S(1)}) fusion(pred[64,8192]{1,0:T(8,128)(4,1)S(1)} %broadcast_compare_fusion.1, bf16[8192,1,128]{2,0,1:T(8,128)(2,1)} %get-tuple-element.102, bf16[256,1024]{1,0:T(8,128)(2,1)} %get-tuple-element.103), kind=kOutput, calls=%fused_computation.24 | convolution fusion | flops 1086324224 | bytes 19531776 | tf_op jit(solution)/shard_map/cond/branch_1_fun/bgrd,kgd->grbk/dot_general | solution.py:164
  302.2 4.7 %fusion.30 = f32[1,8,64,128]{3,2,1,0:T(8,128)S(1)} fusion(bf16[8192,1,128]{2,0,1:T(8,128)(2,1)S(1)} %copy-done.3, f32[8192,64,8]{0,1,2:T(8,128)S(1)} %get-tuple-element.181, f32[8,64]{1,0:T(8,128)S(1)} %broadcast_maximum_fusion.1, pred[64,8192]{1,0:T(8,128)(4,1)S(1)} %broadcast_compare_fusion.1), kind=kOutput, calls=%fused_computation.33 | convolution fusion | flops 1094713344 | bytes 19662848 | tf_op jit(solution)/shard_map/cond/branch_1_fun/grbk,kgd->grbd/dot_general | solution.py:177
  306.9 5.5 %fusion.22 = f32[8,64]{1,0:T(8,128)S(1)} fusion(f32[8192,64,8]{0,1,2:T(8,128)S(1)} %get-tuple-element.181, f32[8,64]{1,0:T(8,128)S(1)} %broadcast_maximum_fusion.1, pred[64,8192]{1,0:T(8,128)(4,1)S(1)} %broadcast_compare_fusion.1), kind=kLoop, calls=%fused_computation.26 | loop fusion | flops 20971008 | bytes 17305600 | tf_op jit(solution)/shard_map/cond/branch_1_fun/reduce_sum | solution.py:176
  312.4 15.8 %conditional.6 = (f32[1,8,64]{2,1,0:T(8,128)S(1)}, f32[1,8,64,128]{3,2,1,0:T(8,128)S(1)}) conditional(s32[]{:T(128)} %bitcast.77, () %tuple.51, (s32[8192]{0:T(1024)S(1)}, s32[256]{0:T(256)S(1)}, bf16[8192,1,128]{2,0,1:T(8,128)(2,1)}, bf16[256,1024]{1,0:T(8,128)(2,1)}, bf16[8192,1,128]{2,0,1:T(8,128)(2,1)}) %tuple.111), branch_computations={%region_14.15_spmd, %region_15.18_spmd} | conditional | flops 2202533376 | bytes 65450796 | solution.py:189
  312.9 4.9 %fusion.40 = (f32[8,64]{1,0:T(8,128)S(1)}, f32[8192,64,8]{0,1,2:T(8,128)S(1)}) fusion(pred[64,8192]{1,0:T(8,128)(4,1)S(1)} %broadcast_compare_fusion.2, bf16[8192,1,128]{2,0,1:T(8,128)(2,1)} %get-tuple-element.107, bf16[256,1024]{1,0:T(8,128)(2,1)} %get-tuple-element.108), kind=kOutput, calls=%fused_computation.44 | convolution fusion | flops 1086324224 | bytes 19531776 | tf_op jit(solution)/shard_map/cond/branch_1_fun/bgrd,kgd->grbk/dot_general | solution.py:164
  317.8 4.8 %fusion.50 = f32[1,8,64,128]{3,2,1,0:T(8,128)S(1)} fusion(bf16[8192,1,128]{2,0,1:T(8,128)(2,1)S(1)} %copy-done.4, f32[8192,64,8]{0,1,2:T(8,128)S(1)} %get-tuple-element.183, f32[8,64]{1,0:T(8,128)S(1)} %broadcast_maximum_fusion.2, pred[64,8192]{1,0:T(8,128)(4,1)S(1)} %broadcast_compare_fusion.2), kind=kOutput, calls=%fused_computation.53 | convolution fusion | flops 1094713344 | bytes 19662848 | tf_op jit(solution)/shard_map/cond/branch_1_fun/grbk,kgd->grbd/dot_general | solution.py:177
  322.7 5.5 %fusion.42 = f32[8,64]{1,0:T(8,128)S(1)} fusion(f32[8192,64,8]{0,1,2:T(8,128)S(1)} %get-tuple-element.183, f32[8,64]{1,0:T(8,128)S(1)} %broadcast_maximum_fusion.2, pred[64,8192]{1,0:T(8,128)(4,1)S(1)} %broadcast_compare_fusion.2), kind=kLoop, calls=%fused_computation.46 | loop fusion | flops 20971008 | bytes 17305600 | tf_op jit(solution)/shard_map/cond/branch_1_fun/reduce_sum | solution.py:176
  328.1 15.5 %conditional.7 = (f32[1,8,64]{2,1,0:T(8,128)S(1)}, f32[1,8,64,128]{3,2,1,0:T(8,128)S(1)}) conditional(s32[]{:T(128)} %bitcast.78, () %tuple.52, (s32[8192]{0:T(1024)S(1)}, s32[256]{0:T(256)S(1)}, bf16[8192,1,128]{2,0,1:T(8,128)(2,1)}, bf16[256,1024]{1,0:T(8,128)(2,1)}, bf16[8192,1,128]{2,0,1:T(8,128)(2,1)}) %tuple.112), branch_computations={%region_18.19_spmd, %region_19.22_spmd} | conditional | flops 2202533376 | bytes 65450796 | solution.py:189
  328.6 4.9 %fusion.60 = (f32[8,64]{1,0:T(8,128)S(1)}, f32[8192,64,8]{0,1,2:T(8,128)S(1)}) fusion(pred[64,8192]{1,0:T(8,128)(4,1)S(1)} %broadcast_compare_fusion.3, bf16[8192,1,128]{2,0,1:T(8,128)(2,1)} %get-tuple-element.112, bf16[256,1024]{1,0:T(8,128)(2,1)} %get-tuple-element.113), kind=kOutput, calls=%fused_computation.64 | convolution fusion | flops 1086324224 | bytes 19531776 | tf_op jit(solution)/shard_map/cond/branch_1_fun/bgrd,kgd->grbk/dot_general | solution.py:164
  333.5 4.7 %fusion.70 = f32[1,8,64,128]{3,2,1,0:T(8,128)S(1)} fusion(bf16[8192,1,128]{2,0,1:T(8,128)(2,1)S(1)} %copy-done.5, f32[8192,64,8]{0,1,2:T(8,128)S(1)} %get-tuple-element.185, f32[8,64]{1,0:T(8,128)S(1)} %broadcast_maximum_fusion.3, pred[64,8192]{1,0:T(8,128)(4,1)S(1)} %broadcast_compare_fusion.3), kind=kOutput, calls=%fused_computation.73 | convolution fusion | flops 1094713344 | bytes 19662848 | tf_op jit(solution)/shard_map/cond/branch_1_fun/grbk,kgd->grbd/dot_general | solution.py:177
  338.1 5.5 %fusion.62 = f32[8,64]{1,0:T(8,128)S(1)} fusion(f32[8192,64,8]{0,1,2:T(8,128)S(1)} %get-tuple-element.185, f32[8,64]{1,0:T(8,128)S(1)} %broadcast_maximum_fusion.3, pred[64,8192]{1,0:T(8,128)(4,1)S(1)} %broadcast_compare_fusion.3), kind=kLoop, calls=%fused_computation.66 | loop fusion | flops 20971008 | bytes 17305600 | tf_op jit(solution)/shard_map/cond/branch_1_fun/reduce_sum | solution.py:176
  344.4 0.9 copy.124
  (71 shorter events, 10.9 us)
Async XLA Ops:
  7.2 118.8 %copy-start.1 = (f32[16]{0:T(128)S(1)}, f32[16]{0:T(128)}, u32[]{:S(2)}) copy-start(f32[16]{0:T(128)} %param.28) | copy-start | bytes 196
  7.2 119.8 %copy-start = (f32[1024]{0:T(1024)S(1)}, f32[1024]{0:T(1024)}, u32[]{:S(2)}) copy-start(f32[1024]{0:T(1024)} %param.31) | copy-start | bytes 12292
  7.2 118.7 %all-gather.10.cloned.1.call-start = ((), (), s32[]{:S(2)}) async-start(), calls=%async_computation.4 | async-start | bytes 8650752 | tf_op jit(solution)/shard_map/all_gather | solution.py:20
  8.2 16.1 %collective-permute-start = (bf16[3,1024]{0,1:T(8,128)(2,1)S(1)}, bf16[3,1024]{0,1:T(8,128)(2,1)S(1)}, u32[]{:S(2)}, u32[]{:S(2)}) collective-permute-start(bf16[3,1024]{0,1:T(8,128)(2,1)S(1)} %copy.76), channel_id=1, source_target_pairs={{0,8},{8,16},{16,24},{24,32},{32,40},{40,48},{48,56},{56,64},{64,7... | collective-permute-start | bytes 18440 | tf_op jit(solution)/shard_map/ppermute | solution.py:14
  12.7 10.1 %collective-permute-start.1 = (bf16[3,1,256]{2,0,1:T(4,128)(2,1)S(1)}, bf16[3,1,256]{2,0,1:T(4,128)(2,1)S(1)}, u32[]{:S(2)}, u32[]{:S(2)}) collective-permute-start(bf16[3,1,256]{2,0,1:T(4,128)(2,1)S(1)} %slice.125), channel_id=1, source_target_pairs={{0,8},{8,16},{16,24},{24,32},{32,40},{40,48},{48,56},{56,64},{64,7... | collective-permute-start | bytes 4616 | tf_op jit(solution)/shard_map/ppermute | solution.py:14
  26.8 176.9 %all-gather.6.cloned.1.call-start = ((), (), s32[]{:S(2)}) async-start(), calls=%async_computation.2 | async-start | bytes 2162688 | tf_op jit(solution)/shard_map/all_gather | solution.py:140
  27.5 254.0 %all-gather.8.cloned.1.call-start = ((), (), s32[]{:S(2)}) async-start(), calls=%async_computation.3 | async-start | bytes 2162688 | tf_op jit(solution)/shard_map/all_gather | solution.py:141
  28.3 317.1 %reduce-scatter.2.cloned.1.call-start = ((), (), s32[]{:S(2)}) async-start(), calls=%async_computation.1 | async-start | bytes 2359296 | tf_op jit(solution)/shard_map/reduce_scatter | solution.py:127
  281.5 5.2 %copy-start.2 = (bf16[8192,1,128]{2,0,1:T(8,128)(2,1)S(1)}, bf16[8192,1,128]{2,0,1:T(8,128)(2,1)}, u32[]{:S(2)}) copy-start(bf16[8192,1,128]{2,0,1:T(8,128)(2,1)} %get-tuple-element.99) | copy-start | bytes 6291460 | tf_op jit(solution)/shard_map/cond
  296.9 5.3 %copy-start.3 = (bf16[8192,1,128]{2,0,1:T(8,128)(2,1)S(1)}, bf16[8192,1,128]{2,0,1:T(8,128)(2,1)}, u32[]{:S(2)}) copy-start(bf16[8192,1,128]{2,0,1:T(8,128)(2,1)} %get-tuple-element.104) | copy-start | bytes 6291460 | tf_op jit(solution)/shard_map/cond
  312.6 5.3 %copy-start.4 = (bf16[8192,1,128]{2,0,1:T(8,128)(2,1)S(1)}, bf16[8192,1,128]{2,0,1:T(8,128)(2,1)}, u32[]{:S(2)}) copy-start(bf16[8192,1,128]{2,0,1:T(8,128)(2,1)} %get-tuple-element.109) | copy-start | bytes 6291460 | tf_op jit(solution)/shard_map/cond
  328.1 5.3 %copy-start.5 = (bf16[8192,1,128]{2,0,1:T(8,128)(2,1)S(1)}, bf16[8192,1,128]{2,0,1:T(8,128)(2,1)}, u32[]{:S(2)}) copy-start(bf16[8192,1,128]{2,0,1:T(8,128)(2,1)} %get-tuple-element.114) | copy-start | bytes 6291460 | tf_op jit(solution)/shard_map/cond
Sparse Core Ops, SparseCore 0:
  26.9 98.9 all-gather.9
  128.5 75.1 all-gather.5
  206.3 75.1 all-gather.7
  284.5 28.6 reduce-scatter.1
where the time goes:
time: 353 us; the launch traced here: 352 us
  waiting for transfers between devices  200 us (57%)
  matrix products  48.7 us (14%)
  blocking collectives  40.3 us (11%)
  other arithmetic  31.6 us (9%)
  between operations  16.4 us (5%)
  starting transfers between devices  7.79 us (2%)
  local copies, waits for them, and re-layouts  6.81 us (2%)
    all_gather x1, waiting for transfers between devices, per_device(): value_block = lax.all_gather(values, 'ctx', axis=0, tiled=True)  77.8 us
    all_gather x1, waiting for transfers between devices, per_device(): key_block = lax.all_gather(attention_keys, 'ctx', axis=0, tiled=True)  66.5 us
    all_gather x1, waiting for transfers between devices, prefix_2(): lax.all_gather(a.astype(kind), axis)  54.2 us
    all_gather x1, blocking collectives, prefix_2(): lax.all_gather(a.astype(kind), axis)  40.3 us
    reduce_sum x4, other arithmetic, update(): new_total = jnp.sum(weights, axis=3)  21.9 us
    dot_general x4, matrix products, update(): jnp.einsum('bgrd,kgd->grbk', query_tile_block, key_head_rows, preferred_e...  19.5 us
    dot_general x4, matrix products, update(): jnp.einsum('grbk,kgd->grbd', weights.astype(jnp.bfloat16), value_head_row...  18.8 us
    ppermute x2, starting transfers between devices, passed_along(): return lax.ppermute(shard, axis, pairs)  7.64 us
  transfers between devices with their start and end apart: 6, of which 3 were waited for; matrix products, arithmetic and copies ran while one was open for 24% of the time, Pallas kernels for 0%

commit v1 on v0

--- a/solution.py
+++ b/solution.py
@@ -137,8 +137,13 @@
     query_heads = queries.reshape(tok_rows, kv_heads, shared_heads, HEAD_SIZE)
     block_rows = tok_rows // 4
     first_key = jnp.int32(0)
-    key_block = lax.all_gather(attention_keys, "ctx", axis=0, tiled=True)
-    value_block = lax.all_gather(values, "ctx", axis=0, tiled=True)
+    key_block, value_block = jnp.split(
+        lax.all_gather(
+            jnp.concatenate([attention_keys, values], axis=1), axis_name="ctx", axis=0, tiled=True
+        ),
+        [attention_keys.shape[1]],
+        axis=1,
+    )
     key_count = key_block.shape[0]
     key_head_rows = key_block.reshape(key_count, kv_heads, HEAD_SIZE)
     value_head_rows = value_block.reshape(key_count, kv_heads, HEAD_SIZE)

time: 353 us -> 284 us (0.80)
  waiting for transfers between devices: 200 us -> 125 us
  local copies, waits for them, and re-layouts: 6.81 us -> 10.6 us
    all_gather x2 -> x1, waiting for transfers between devices: 144 us -> 70.7 us  [per_device(): lax.all_gather(jnp.concatenate([attention_keys, values], axis=1), axis_na...]
    reshape x2 -> x3, local copies, waits for them, and re-layouts: 0.02 us -> 3.81 us  [the longest x1 3.79 us: per_device(): value_head_rows = value_block.reshape(key_count, kv_heads, HEAD_SIZE)]
  transfers between devices with their start and end apart: 6 -> 5, of which waited for: 3 -> 2; matrix products, arithmetic and copies ran while one was open for 24% -> 32% of each run, Pallas kernels for 0% -> 0%
where the time goes in v1:
time: 284 us; the launch traced here: 282 us
  waiting for transfers between devices  125 us (44%)
  matrix products  48.6 us (17%)
  blocking collectives  40.3 us (14%)
  other arithmetic  33.2 us (12%)
  between operations  16.4 us (6%)
  local copies, waits for them, and re-layouts  10.6 us (4%)
  starting transfers between devices  7.76 us (3%)
    all_gather x1, waiting for transfers between devices, per_device(): lax.all_gather(jnp.concatenate([attention_keys, values], axis=1), axis_na...  70.7 us
    all_gather x1, waiting for transfers between devices, prefix_2(): lax.all_gather(a.astype(kind), axis)  54.1 us
    all_gather x1, blocking collectives, prefix_2(): lax.all_gather(a.astype(kind), axis)  40.3 us
    reduce_sum x4, other arithmetic, update(): new_total = jnp.sum(weights, axis=3)  21.9 us
    dot_general x4, matrix products, update(): jnp.einsum('grbk,kgd->grbd', weights.astype(jnp.bfloat16), value_head_row...  19.6 us
    dot_general x4, matrix products, update(): jnp.einsum('bgrd,kgd->grbk', query_tile_block, key_head_rows, preferred_e...  18.6 us
    ppermute x2, starting transfers between devices, passed_along(): return lax.ppermute(shard, axis, pairs)  7.64 us
    dot_general x1, matrix products, per_device(): jnp.dot(normed, out_weight, preferred_element_type=jnp.float32)  7.2 us
  transfers between devices with their start and end apart: 5, of which 2 were waited for; matrix products, arithmetic and copies ran while one was open for 32% of the time, Pallas kernels for 0%

profile of v1, /device:TPU:4, one launch (start us, length us, event | category | flops | bytes accessed | tf_op | source)
XLA Modules:
  0.0 282.3 jit_solution(7875068852998543862)
XLA Ops:
  8.2 3.8 %collective-permute-start = (bf16[3,1024]{0,1:T(8,128)(2,1)S(1)}, bf16[3,1024]{0,1:T(8,128)(2,1)S(1)}, u32[]{:S(2)}, u32[]{:S(2)}) collective-permute-start(bf16[3,1024]{0,1:T(8,128)(2,1)S(1)} %copy.76), channel_id=1, source_target_pairs={{0,8},{8,16},{16,24},{24,32},{32,40},{40,48},{48,56},{56,64},{64,7... | collective-permute-start | bytes 18440 | tf_op jit(solution)/shard_map/ppermute | solution.py:14
  12.7 3.8 %collective-permute-start.1 = (bf16[3,1,256]{2,0,1:T(4,128)(2,1)S(1)}, bf16[3,1,256]{2,0,1:T(4,128)(2,1)S(1)}, u32[]{:S(2)}, u32[]{:S(2)}) collective-permute-start(bf16[3,1,256]{2,0,1:T(4,128)(2,1)S(1)} %slice.125), channel_id=1, source_target_pairs={{0,8},{8,16},{16,24},{24,32},{32,40},{40,48},{48,56},{56,64},{64,7... | collective-permute-start | bytes 4616 | tf_op jit(solution)/shard_map/ppermute | solution.py:14
  19.0 0.9 slice_convert_fusion.3
  21.6 1.2 copy.77
  22.8 1.4 multiply_convert_fusion.7
  24.3 1.5 fusion.96
  25.7 1.0 convolution_convert_fusion.1
  26.8 1.5 pad_maximum_fusion.2
  28.5 40.3 %all-gather = bf16[32,16,1]{1,2,0:T(2,128)(2,1)S(1)} all-gather(bf16[1,16,1]{1,2,0:T(2,128)(2,1)S(1)} %slice.213), channel_id=2, replica_groups=mesh['ctx'=32,'tp'=8] {'ctx'}, dimensions={0}, use_global_device_ids=true | all-gather | bytes 1056 | tf_op jit(solution)/shard_map/all_gather | solution.py:20
  69.0 1.2 copy.88
  70.5 1.4 fusion.87
  71.9 54.1 %all-gather.7.cloned.1.call-done = bf16[512,64,128]{2,1,0:T(8,128)(2,1)} async-done(((bf16[16,64,128]{2,1,0:T(8,128)(2,1)}), bf16[512,64,128]{2,1,0:T(8,128)(2,1)}) %all-gather.7.cloned.1.call-update) | async-done | bytes 8388624 | tf_op jit(solution)/shard_map/all_gather | solution.py:20
  127.1 7.2 %convolution_convert_fusion = bf16[256,4096]{1,0:T(8,128)(2,1)} fusion(bf16[1024,4096]{1,0:T(8,128)(2,1)} %param.32, f32[256,1024]{0,1:T(8,128)S(1)} %get-tuple-element.171, f32[1024]{0:T(1024)S(1)} %copy-done, f32[256]{0:T(256)S(1)} %add_rsqrt_fusion), kind=kOutput, calls=%fused_computation.82 | convolution fusion | flops 2149318656 | bytes 11539456 | tf_op jit(solution)/shard_map/dot_general | solution.py:128
  137.4 70.7 %all-gather.5.cloned.1.call-done = bf16[8192,256]{1,0:T(8,128)(2,1)} async-done(((bf16[256,256]{1,0:T(8,128)(2,1)}), bf16[8192,256]{1,0:T(8,128)(2,1)}) %all-gather.5.cloned.1.call-update) | async-done | bytes 4194320 | tf_op jit(solution)/shard_map/all_gather | solution.py:141
  208.1 3.8 %slice_bitcast_fusion.4 = (bf16[8192,1,128]{2,0,1:T(8,128)(2,1)S(1)}, bf16[8192,1,128]{2,0,1:T(8,128)(2,1)}) fusion(bf16[8192,256]{1,0:T(8,128)(2,1)} %all-gather.5.cloned.1.call-done), kind=kLoop, calls=%fused_computation.85 | loop fusion | bytes 8388608 | tf_op jit(solution)/shard_map/reshape | solution.py:149
  211.9 15.6 %conditional.4 = (f32[1,8,64]{2,1,0:T(8,128)S(1)}, f32[1,8,64,128]{3,2,1,0:T(8,128)S(1)}) conditional(s32[]{:T(128)} %bitcast.73, () %tuple.48, (s32[8192]{0:T(1024)S(1)}, s32[256]{0:T(256)S(1)}, bf16[8192,1,128]{2,0,1:T(8,128)(2,1)}, bf16[256,1024]{1,0:T(8,128)(2,1)S(1)}, bf16[8192,1,128]{2,0,1:T(8,128)(2,1)S(1)}) %tuple.104), branch_computations={%region_6.7_spmd, %region_7.10_spmd} | conditional | flops 2202533376 | bytes 57062160 | solution.py:194
  212.4 4.6 %fusion = (f32[8,64]{1,0:T(8,128)S(1)}, f32[8192,64,8]{0,1,2:T(8,128)S(1)}) fusion(pred[64,8192]{1,0:T(8,128)(4,1)S(1)} %broadcast_compare_fusion, bf16[8192,1,128]{2,0,1:T(8,128)(2,1)} %get-tuple-element.97, bf16[256,1024]{1,0:T(8,128)(2,1)S(1)} %get-tuple-element.98), kind=kOutput, calls=%fused_computation.4 | convolution fusion | flops 1086324224 | bytes 19531776 | tf_op jit(solution)/shard_map/cond/branch_1_fun/bgrd,kgd->grbk/dot_general | solution.py:169
  217.1 4.9 %fusion.10 = f32[1,8,64,128]{3,2,1,0:T(8,128)S(1)} fusion(bf16[8192,1,128]{2,0,1:T(8,128)(2,1)S(1)} %get-tuple-element.99, f32[8192,64,8]{0,1,2:T(8,128)S(1)} %get-tuple-element.179, f32[8,64]{1,0:T(8,128)S(1)} %broadcast_maximum_fusion, pred[64,8192]{1,0:T(8,128)(4,1)S(1)} %broadcast_compare_fusion), kind=kOutput, calls=%fused_computation.13 | convolution fusion | flops 1094713344 | bytes 19662848 | tf_op jit(solution)/shard_map/cond/branch_1_fun/grbk,kgd->grbd/dot_general | solution.py:182
  222.0 5.5 %fusion.2 = f32[8,64]{1,0:T(8,128)S(1)} fusion(f32[8192,64,8]{0,1,2:T(8,128)S(1)} %get-tuple-element.179, f32[8,64]{1,0:T(8,128)S(1)} %broadcast_maximum_fusion, pred[64,8192]{1,0:T(8,128)(4,1)S(1)} %broadcast_compare_fusion), kind=kLoop, calls=%fused_computation.6 | loop fusion | flops 20971008 | bytes 17305600 | tf_op jit(solution)/shard_map/cond/branch_1_fun/reduce_sum | solution.py:181
  227.5 15.5 %conditional.5 = (f32[1,8,64]{2,1,0:T(8,128)S(1)}, f32[1,8,64,128]{3,2,1,0:T(8,128)S(1)}) conditional(s32[]{:T(128)} %bitcast.76, () %tuple.50, (s32[8192]{0:T(1024)S(1)}, s32[256]{0:T(256)S(1)}, bf16[8192,1,128]{2,0,1:T(8,128)(2,1)}, bf16[256,1024]{1,0:T(8,128)(2,1)S(1)}, bf16[8192,1,128]{2,0,1:T(8,128)(2,1)S(1)}) %tuple.105), branch_computations={%region_10.11_spmd, %region_11.14_spmd} | conditional | flops 2202533376 | bytes 57062160 | solution.py:194
  227.9 4.7 %fusion.20 = (f32[8,64]{1,0:T(8,128)S(1)}, f32[8192,64,8]{0,1,2:T(8,128)S(1)}) fusion(pred[64,8192]{1,0:T(8,128)(4,1)S(1)} %broadcast_compare_fusion.1, bf16[8192,1,128]{2,0,1:T(8,128)(2,1)} %get-tuple-element.102, bf16[256,1024]{1,0:T(8,128)(2,1)S(1)} %get-tuple-element.103), kind=kOutput, calls=%fused_computation.24 | convolution fusion | flops 1086324224 | bytes 19531776 | tf_op jit(solution)/shard_map/cond/branch_1_fun/bgrd,kgd->grbk/dot_general | solution.py:169
  232.6 4.9 %fusion.30 = f32[1,8,64,128]{3,2,1,0:T(8,128)S(1)} fusion(bf16[8192,1,128]{2,0,1:T(8,128)(2,1)S(1)} %get-tuple-element.104, f32[8192,64,8]{0,1,2:T(8,128)S(1)} %get-tuple-element.181, f32[8,64]{1,0:T(8,128)S(1)} %broadcast_maximum_fusion.1, pred[64,8192]{1,0:T(8,128)(4,1)S(1)} %broadcast_compare_fusion.1), kind=kOutput, calls=%fused_computation.33 | convolution fusion | flops 1094713344 | bytes 19662848 | tf_op jit(solution)/shard_map/cond/branch_1_fun/grbk,kgd->grbd/dot_general | solution.py:182
  237.5 5.5 %fusion.22 = f32[8,64]{1,0:T(8,128)S(1)} fusion(f32[8192,64,8]{0,1,2:T(8,128)S(1)} %get-tuple-element.181, f32[8,64]{1,0:T(8,128)S(1)} %broadcast_maximum_fusion.1, pred[64,8192]{1,0:T(8,128)(4,1)S(1)} %broadcast_compare_fusion.1), kind=kLoop, calls=%fused_computation.26 | loop fusion | flops 20971008 | bytes 17305600 | tf_op jit(solution)/shard_map/cond/branch_1_fun/reduce_sum | solution.py:181
  242.9 15.6 %conditional.6 = (f32[1,8,64]{2,1,0:T(8,128)S(1)}, f32[1,8,64,128]{3,2,1,0:T(8,128)S(1)}) conditional(s32[]{:T(128)} %bitcast.77, () %tuple.51, (s32[8192]{0:T(1024)S(1)}, s32[256]{0:T(256)S(1)}, bf16[8192,1,128]{2,0,1:T(8,128)(2,1)}, bf16[256,1024]{1,0:T(8,128)(2,1)S(1)}, bf16[8192,1,128]{2,0,1:T(8,128)(2,1)S(1)}) %tuple.106), branch_computations={%region_14.15_spmd, %region_15.18_spmd} | conditional | flops 2202533376 | bytes 57062160 | solution.py:194
  243.5 4.7 %fusion.40 = (f32[8,64]{1,0:T(8,128)S(1)}, f32[8192,64,8]{0,1,2:T(8,128)S(1)}) fusion(pred[64,8192]{1,0:T(8,128)(4,1)S(1)} %broadcast_compare_fusion.2, bf16[8192,1,128]{2,0,1:T(8,128)(2,1)} %get-tuple-element.107, bf16[256,1024]{1,0:T(8,128)(2,1)S(1)} %get-tuple-element.108), kind=kOutput, calls=%fused_computation.44 | convolution fusion | flops 1086324224 | bytes 19531776 | tf_op jit(solution)/shard_map/cond/branch_1_fun/bgrd,kgd->grbk/dot_general | solution.py:169
  248.2 4.9 %fusion.50 = f32[1,8,64,128]{3,2,1,0:T(8,128)S(1)} fusion(bf16[8192,1,128]{2,0,1:T(8,128)(2,1)S(1)} %get-tuple-element.109, f32[8192,64,8]{0,1,2:T(8,128)S(1)} %get-tuple-element.183, f32[8,64]{1,0:T(8,128)S(1)} %broadcast_maximum_fusion.2, pred[64,8192]{1,0:T(8,128)(4,1)S(1)} %broadcast_compare_fusion.2), kind=kOutput, calls=%fused_computation.53 | convolution fusion | flops 1094713344 | bytes 19662848 | tf_op jit(solution)/shard_map/cond/branch_1_fun/grbk,kgd->grbd/dot_general | solution.py:182
  253.1 5.5 %fusion.42 = f32[8,64]{1,0:T(8,128)S(1)} fusion(f32[8192,64,8]{0,1,2:T(8,128)S(1)} %get-tuple-element.183, f32[8,64]{1,0:T(8,128)S(1)} %broadcast_maximum_fusion.2, pred[64,8192]{1,0:T(8,128)(4,1)S(1)} %broadcast_compare_fusion.2), kind=kLoop, calls=%fused_computation.46 | loop fusion | flops 20971008 | bytes 17305600 | tf_op jit(solution)/shard_map/cond/branch_1_fun/reduce_sum | solution.py:181
  258.6 15.5 %conditional.7 = (f32[1,8,64]{2,1,0:T(8,128)S(1)}, f32[1,8,64,128]{3,2,1,0:T(8,128)S(1)}) conditional(s32[]{:T(128)} %bitcast.78, () %tuple.52, (s32[8192]{0:T(1024)S(1)}, s32[256]{0:T(256)S(1)}, bf16[8192,1,128]{2,0,1:T(8,128)(2,1)}, bf16[256,1024]{1,0:T(8,128)(2,1)S(1)}, bf16[8192,1,128]{2,0,1:T(8,128)(2,1)S(1)}) %tuple.107), branch_computations={%region_18.19_spmd, %region_19.22_spmd} | conditional | flops 2202533376 | bytes 57062160 | solution.py:194
  259.0 4.6 %fusion.60 = (f32[8,64]{1,0:T(8,128)S(1)}, f32[8192,64,8]{0,1,2:T(8,128)S(1)}) fusion(pred[64,8192]{1,0:T(8,128)(4,1)S(1)} %broadcast_compare_fusion.3, bf16[8192,1,128]{2,0,1:T(8,128)(2,1)} %get-tuple-element.112, bf16[256,1024]{1,0:T(8,128)(2,1)S(1)} %get-tuple-element.113), kind=kOutput, calls=%fused_computation.64 | convolution fusion | flops 1086324224 | bytes 19531776 | tf_op jit(solution)/shard_map/cond/branch_1_fun/bgrd,kgd->grbk/dot_general | solution.py:169
  263.7 4.9 %fusion.70 = f32[1,8,64,128]{3,2,1,0:T(8,128)S(1)} fusion(bf16[8192,1,128]{2,0,1:T(8,128)(2,1)S(1)} %get-tuple-element.114, f32[8192,64,8]{0,1,2:T(8,128)S(1)} %get-tuple-element.185, f32[8,64]{1,0:T(8,128)S(1)} %broadcast_maximum_fusion.3, pred[64,8192]{1,0:T(8,128)(4,1)S(1)} %broadcast_compare_fusion.3), kind=kOutput, calls=%fused_computation.73 | convolution fusion | flops 1094713344 | bytes 19662848 | tf_op jit(solution)/shard_map/cond/branch_1_fun/grbk,kgd->grbd/dot_general | solution.py:182
  268.6 5.5 %fusion.62 = f32[8,64]{1,0:T(8,128)S(1)} fusion(f32[8192,64,8]{0,1,2:T(8,128)S(1)} %get-tuple-element.185, f32[8,64]{1,0:T(8,128)S(1)} %broadcast_maximum_fusion.3, pred[64,8192]{1,0:T(8,128)(4,1)S(1)} %broadcast_compare_fusion.3), kind=kLoop, calls=%fused_computation.66 | loop fusion | flops 20971008 | bytes 17305600 | tf_op jit(solution)/shard_map/cond/branch_1_fun/reduce_sum | solution.py:181
  274.8 0.9 copy.124
  (64 shorter events, 10.4 us)
Async XLA Ops:
  7.2 118.9 %copy-start.1 = (f32[16]{0:T(128)S(1)}, f32[16]{0:T(128)}, u32[]{:S(2)}) copy-start(f32[16]{0:T(128)} %param.28) | copy-start | bytes 196
  7.2 119.9 %copy-start = (f32[1024]{0:T(1024)S(1)}, f32[1024]{0:T(1024)}, u32[]{:S(2)}) copy-start(f32[1024]{0:T(1024)} %param.31) | copy-start | bytes 12292
  7.2 118.8 %all-gather.7.cloned.1.call-start = ((), (), s32[]{:S(2)}) async-start(), calls=%async_computation.3 | async-start | bytes 8650752 | tf_op jit(solution)/shard_map/all_gather | solution.py:20
  8.2 16.1 %collective-permute-start = (bf16[3,1024]{0,1:T(8,128)(2,1)S(1)}, bf16[3,1024]{0,1:T(8,128)(2,1)S(1)}, u32[]{:S(2)}, u32[]{:S(2)}) collective-permute-start(bf16[3,1024]{0,1:T(8,128)(2,1)S(1)} %copy.76), channel_id=1, source_target_pairs={{0,8},{8,16},{16,24},{24,32},{32,40},{40,48},{48,56},{56,64},{64,7... | collective-permute-start | bytes 18440 | tf_op jit(solution)/shard_map/ppermute | solution.py:14
  12.7 10.1 %collective-permute-start.1 = (bf16[3,1,256]{2,0,1:T(4,128)(2,1)S(1)}, bf16[3,1,256]{2,0,1:T(4,128)(2,1)S(1)}, u32[]{:S(2)}, u32[]{:S(2)}) collective-permute-start(bf16[3,1,256]{2,0,1:T(4,128)(2,1)S(1)} %slice.125), channel_id=1, source_target_pairs={{0,8},{8,16},{16,24},{24,32},{32,40},{40,48},{48,56},{56,64},{64,7... | collective-permute-start | bytes 4616 | tf_op jit(solution)/shard_map/ppermute | solution.py:14
  26.8 181.3 %all-gather.5.cloned.1.call-start = ((), (), s32[]{:S(2)}) async-start(), calls=%async_computation.2 | async-start | bytes 4325376 | tf_op jit(solution)/shard_map/all_gather | solution.py:141
  28.4 247.3 %reduce-scatter.2.cloned.1.call-start = ((), (), s32[]{:S(2)}) async-start(), calls=%async_computation.1 | async-start | bytes 2359296 | tf_op jit(solution)/shard_map/reduce_scatter | solution.py:127
  126.1 85.8 %copy-start.2 = (bf16[256,1024]{1,0:T(8,128)(2,1)S(1)}, bf16[256,1024]{1,0:T(8,128)(2,1)}, u32[]{:S(2)}) copy-start(bf16[256,1024]{1,0:T(8,128)(2,1)} %param.33) | copy-start | bytes 1572868
Sparse Core Ops, SparseCore 0:
  26.9 99.0 all-gather.6
  129.2 78.8 all-gather.4
  211.2 28.2 reduce-scatter.1
